TPU v7x, 512 devices: a whole 4x4x16 slice. The times are simulated.
512 devices in a mesh: tile: 128 (over x, z, core), rep: 4 (over y).
Axes of the slice: x: 4, y: 4, z: 16, core: 2. Of those that a mesh axis runs over, the one named last changes fastest.
Arguments:
- embedding: bfloat16 [2048, 64, 256], P('tile'), may hold values from -6 to 6
- prompt_tile: int32 [65536, 1], P(('tile', 'rep')), may hold values from 0 to 127; in each aligned block of 128 rows (0 to 127, 128 to 255, ...) at most 2 rows name the same one
- crop_row: int32 [65536], P(('tile', 'rep')), may hold values from 0 to 15
- crop_col: int32 [65536], P(('tile', 'rep')), may hold values from 0 to 60
- points: int32 [65536, 2], P(('tile', 'rep')), may hold values from 0 to 15
- confidence: int32 [65536], P(('tile', 'rep')), may hold values from 1 to 4
- pe_matrix: float32 [2, 128], replicated, may hold values from -5 to 5
- point_embed: float32 [256], replicated, may hold values from -5 to 5
- w_one: bfloat16 [256, 256], replicated, may hold values from -0.375 to 0.375
- w_two: bfloat16 [256, 256], replicated, may hold values from -0.375 to 0.375
- w_three: bfloat16 [256, 32], replicated, may hold values from -0.375 to 0.375
- conv_one: bfloat16 [256, 256], replicated, may hold values from -0.375 to 0.375
- conv_two: bfloat16 [64, 128], replicated, may hold values from -0.75 to 0.75
Outputs:
- mask_sum: float32 [8192, 256], P('tile')
Inputs may be any that keep to these rules, and one draw needn't show every extreme that they name: `prompt_tile`: among the prompts of one device no strip is named more than 2 times, and some device names some strip exactly 2 times.
All inputs are finite; a program needn't handle non-finite values.
Results may differ from a plain program's by a relative error of at most 0.0049.
Values may be sent and summed in bfloat16 or wider, within the bound.
No kernel may reach another device: no remote copies, remote signals or barrier semaphores. Data moves between devices by JAX's collectives and lax.ppermute only.
A program may use at most 64 MiB of HBM per device.

v0:
```python
import math
import jax
import jax.numpy as jnp
from jax import lax
from jax.sharding import PartitionSpec as P

CK = 4


def shifted(value, axis, steps):
    count = lax.axis_size(axis)
    leading, last = (max(0, -steps), min(count, count - steps))
    return lax.ppermute(value, axis, [(source, source + steps) for source in range(leading, last)])


def prompt_heads(points, pe_matrix, point_embed, w_one, w_two, w_three):
    coords = (points.astype(jnp.float32) + 0.5) / (4.0 * CK) * 2.0 - 1.0
    angles = (coords[:, 0:1] * pe_matrix[0][None, :] + coords[:, 1:2] * pe_matrix[1][None, :]) * (
        2.0 * math.pi
    )
    tokens = (
        jnp.concatenate([jnp.sin(angles), jnp.cos(angles)], axis=1) + point_embed[None, :]
    ).astype(jnp.bfloat16)
    hidden_one = jax.nn.relu(jnp.dot(tokens, w_one, preferred_element_type=jnp.float32)).astype(
        jnp.bfloat16
    )
    hidden_two = jax.nn.relu(jnp.dot(hidden_one, w_two, preferred_element_type=jnp.float32)).astype(
        jnp.bfloat16
    )
    return jnp.dot(hidden_two, w_three, preferred_element_type=jnp.float32).astype(jnp.bfloat16)


def mask_terms(crop_cells, head_rows, scale_rows, conv_one, conv_two):
    amount, crop_side, channels = (crop_cells.shape[0], crop_cells.shape[1], crop_cells.shape[3])
    mid_width = conv_one.shape[1] // 4
    narrow = conv_two.shape[1] // 4
    first_up = jnp.dot(
        crop_cells.reshape(amount * crop_side * crop_side, channels),
        conv_one,
        preferred_element_type=jnp.float32,
    )
    first_up = first_up.reshape(amount * crop_side * crop_side * 4, mid_width)
    centre = first_up - jnp.mean(first_up, axis=1, keepdims=True)
    normed = centre * lax.rsqrt(jnp.mean(centre * centre, axis=1, keepdims=True) + 1e-06)
    active = jax.nn.gelu(normed, approximate=False).astype(jnp.bfloat16)
    second = jnp.dot(active, conv_two, preferred_element_type=jnp.float32)
    upscaled = (
        jax.nn.gelu(second, approximate=False)
        .astype(jnp.bfloat16)
        .reshape(amount, crop_side * crop_side * 16, narrow)
    )
    logits = jnp.einsum("nqc,nc->nq", upscaled, head_rows, preferred_element_type=jnp.float32)
    logits = logits.reshape(amount, crop_side, crop_side, 2, 2, 2, 2).transpose(0, 1, 3, 5, 2, 4, 6)
    logits = logits.reshape(amount, 4 * crop_side, 4 * crop_side)
    return (logits * scale_rows[:, None, None]).astype(jnp.bfloat16)


def terms_in_blocks(crop_cells, head_rows, scale_rows, conv_one, conv_two):
    amount = crop_cells.shape[0]
    block_size = 64
    groups = amount // block_size

    def one_block(group_in):
        return mask_terms(group_in[0], group_in[1], group_in[2], conv_one, conv_two)

    result = lax.map(
        one_block,
        (
            crop_cells.reshape((groups, block_size) + crop_cells.shape[1:]),
            head_rows.reshape(groups, block_size, head_rows.shape[1]),
            scale_rows.reshape(groups, block_size),
        ),
    )
    return result.reshape((amount,) + result.shape[2:])


def cut_crops(extended, row_starts, col_starts):
    height, width, channels = (extended.shape[0], extended.shape[1], extended.shape[2])
    offsets = jnp.arange(CK, dtype=jnp.int32)
    cell_rows = row_starts.astype(jnp.int32)[:, None, None] + offsets[None, :, None]
    cell_cols = col_starts.astype(jnp.int32)[:, None, None] + offsets[None, None, :]
    cell_index = (cell_rows * width + cell_cols).reshape(-1)
    picked = jnp.take(extended.reshape(height * width, channels), cell_index, axis=0)
    return picked.reshape(row_starts.shape[0], CK, CK, channels)


def place_patches(patches, row_starts, col_starts, height, breadth):
    amount, patch_side = (patches.shape[0], patches.shape[1])
    block_size = 64
    groups = amount // block_size
    offsets = jnp.arange(patch_side, dtype=jnp.int32)
    canvas_rows = jnp.arange(height, dtype=jnp.int32)
    canvas_cols = jnp.arange(breadth, dtype=jnp.int32)

    def add_block(canvas, block_in):
        patch_in, row_at, col_at = block_in
        col_table = (
            4 * col_at[:, None, None] + offsets[None, :, None] == canvas_cols[None, None, :]
        ).astype(jnp.bfloat16)
        placed = jnp.einsum(
            "byx,bxs->bys", patch_in, col_table, preferred_element_type=jnp.float32
        ).astype(jnp.bfloat16)
        row_table = (
            4 * row_at[:, None, None] + offsets[None, :, None] == canvas_rows[None, None, :]
        ).astype(jnp.bfloat16)
        added = jnp.einsum(
            "kr,ks->rs",
            row_table.reshape(block_size * patch_side, height),
            placed.reshape(block_size * patch_side, breadth),
            preferred_element_type=jnp.float32,
        )
        return (canvas + added, None)

    canvas, unused = lax.scan(
        add_block,
        jnp.zeros((height, breadth), jnp.float32),
        (
            patches.reshape(groups, block_size, patch_side, patch_side),
            row_starts.reshape(groups, block_size),
            col_starts.reshape(groups, block_size),
        ),
    )
    return canvas


def on_device(
    embedding,
    prompt_tile,
    crop_row,
    crop_col,
    points,
    confidence,
    pe_matrix,
    point_embed,
    w_one,
    w_two,
    w_three,
    conv_one,
    conv_two,
):
    tile_count = lax.axis_size("tile")
    strip_height = embedding.shape[0]
    breadth = 4 * embedding.shape[1]
    prompt_count = prompt_tile.shape[0]
    slot_most = max(2, 2 * prompt_count // tile_count)
    slot_total = tile_count * slot_most
    dynamic_heads = prompt_heads(points, pe_matrix, point_embed, w_one, w_two, w_three)
    head_width = dynamic_heads.shape[1]
    target = prompt_tile[:, 0]
    onehot = (target[:, None] == jnp.arange(tile_count, dtype=jnp.int32)[None, :]).astype(jnp.int32)
    earlier = jnp.cumsum(onehot, axis=0) - onehot
    rank_in = jnp.sum(earlier * onehot, axis=1)
    slot_index = target * slot_most + rank_in
    request = jnp.stack([crop_row, crop_col, confidence], axis=1)
    request_slots = (
        jnp.zeros((slot_total, 3), jnp.int32)
        .at[slot_index]
        .set(request)
        .reshape(tile_count, slot_most, 3)
    )
    rows_below = shifted(embedding[: CK - 1], "tile", -1)
    extended = jnp.concatenate([embedding, rows_below], axis=0)
    head_slots = jnp.zeros((slot_total, head_width), jnp.bfloat16).at[slot_index].set(dynamic_heads)
    head_slots = head_slots.reshape(tile_count, slot_most, head_width)
    head_in = lax.all_to_all(head_slots, "tile", split_axis=0, concat_axis=0, tiled=True)
    request_in = lax.all_to_all(request_slots, "tile", split_axis=0, concat_axis=0, tiled=True)
    sources = request_in.shape[0]
    per_source = request_in.shape[1]
    flat_request = request_in.reshape(sources * per_source, 3)
    crop_cells = cut_crops(extended, flat_request[:, 0], flat_request[:, 1])
    patches = terms_in_blocks(
        crop_cells,
        head_in.reshape(sources * per_source, head_width),
        flat_request[:, 2].astype(jnp.float32) / 4.0,
        conv_one,
        conv_two,
    )
    patch_slots = patches.reshape(sources, per_source, 4 * CK, 4 * CK)
    owner_flat = request_in.reshape(slot_total, 3)
    canvas = place_patches(
        patch_slots.reshape(slot_total, 4 * CK, 4 * CK),
        owner_flat[:, 0],
        owner_flat[:, 1],
        4 * strip_height + 4 * CK - 4,
        breadth,
    )
    summed = lax.psum(canvas, "rep")
    spilled = shifted(summed[4 * strip_height :], "tile", 1)
    return summed[: 4 * strip_height] + jnp.pad(
        spilled, ((0, 4 * strip_height - spilled.shape[0]), (0, 0))
    )


def solution(mesh):
    return jax.shard_map(
        on_device,
        mesh=mesh,
        in_specs=(
            P("tile", None, None),
            P(("tile", "rep"), None),
            P(("tile", "rep")),
            P(("tile", "rep")),
            P(("tile", "rep"), None),
            P(("tile", "rep")),
            P(),
            P(),
            P(),
            P(),
            P(),
            P(),
            P(),
        ),
        out_specs=P("tile", None),
        check_vma=False,
    )
```

profile of v0, /device:TPU:2, one launch (start us, length us, event | category | flops | bytes accessed | tf_op | source)
XLA Modules:
  0.0 257.4 jit_solution(17116012527974906901)
XLA Ops:
  9.8 1.5 scatter_custom_fusion
  11.3 19.5 %all-to-all-start = ((s32[128,2,3]{2,1,0:T(2,128)}), s32[128,2,3]{2,1,0:T(2,128)S(1)}, u32[]{:S(2)}, u32[]{:S(2)}) async-start(s32[128,2,3]{2,1,0:T(2,128)} %bitcast.13), calls=%async_computation | async-start | bytes 262144 | tf_op jit(solution)/shard_map/all_to_all | solution.py:166
  31.8 4.3 %collective-permute-start = (bf16[3,64,256]{2,1,0:T(8,128)(2,1)S(1)}, bf16[3,64,256]{2,1,0:T(8,128)(2,1)S(1)}, u32[]{:S(2)}, u32[]{:S(2)}) collective-permute-start(bf16[3,64,256]{2,1,0:T(8,128)(2,1)S(1)} %slice.36), channel_id=1, source_target_pairs={{4,0},{8,4},{12,8},{16,12},{20,16},{24,20},{28,24},{32,28},{36,32}... | collective-permute-start | bytes 294920 | tf_op jit(solution)/shard_map/ppermute | solution.py:13
  37.9 1.2 fusion.74
  40.1 1.5 scatter_custom_fusion.1
  41.6 6.4 %all-to-all-done = s32[128,2,3]{2,1,0:T(2,128)S(1)} async-done(((s32[128,2,3]{2,1,0:T(2,128)}), s32[128,2,3]{2,1,0:T(2,128)S(1)}, u32[]{:S(2)}, u32[]{:S(2)}) %all-to-all-start) | async-done | bytes 3104 | tf_op jit(solution)/shard_map/all_to_all | solution.py:166
  48.0 8.2 %all-to-all-start.1 = ((bf16[128,2,32]{2,1,0:T(2,128)(2,1)}), bf16[128,2,32]{2,1,0:T(2,128)(2,1)}, u32[]{:S(2)}, u32[]{:S(2)}) async-start(bf16[128,2,32]{2,1,0:T(2,128)(2,1)} %bitcast.23), calls=%async_computation.1 | async-start | bytes 131072 | tf_op jit(solution)/shard_map/all_to_all | solution.py:165
  59.3 14.6 %gather_fusion = bf16[4096,256]{1,0:T(8,128)(2,1)S(1)} fusion(bf16[1216,256]{1,0:T(8,128)(2,1)S(1)} %bitcast.78, s32[4096]{0:T(1024)S(1)} %broadcast_clamp_fusion), kind=kCustom, calls=%fused_computation | custom fusion | bytes 4210688 | tf_op jit(solution)/shard_map/jit(_take)/gather | solution.py:83
  73.9 2.1 gather.7
  76.0 3.4 %broadcast_select_fusion = bf16[4,64,4,4,256]{4,3,2,1,0:T(4,128)(2,1)S(1)} fusion(bf16[4,64,4,4,256]{4,3,2,1,0:T(4,128)(2,1)} %gather.7, pred[4,64,4,4]{3,2,1,0:T(4,128)(4,1)S(1)} %copy.42), kind=kLoop, calls=%fused_computation.104 | loop fusion | flops 1048576 | bytes 4198400 | tf_op jit(solution)/shard_map/jit(_take)/select_n | solution.py:83
  79.4 92.5 %while.22 = (s32[]{:T(128)}, bf16[4,64,16,16]{1,3,2,0:T(8,128)(2,1)}, bf16[4,64,4,4,256]{4,3,2,1,0:T(4,128)(2,1)S(1)}, bf16[256,256]{1,0:T(8,128)(2,1)S(1)}, bf1...) while((s32[]{:T(128)}, ...), condition=%wide.region_7.8_spmd, body=%wide.region_4.7_spmd.sunk | while | flops 255102976 | bytes 30717376 | solution.py:66
  82.0 1.3 multiply_reduce_fusion.3
  83.4 10.8 %fusion.126 = bf16[4096,128]{1,0:T(8,128)(2,1)S(1)} fusion(bf16[64,128]{1,0:T(8,128)(2,1)S(1)} %copy-done.9, f32[4096,64]{1,0:T(8,128)S(1)} %reshape.309, f32[4096]{0:T(1024)S(1)} %add_rsqrt_fusion.2, f32[4096]{0:T(1024)S(1)} %broadcast_multiply_fusion.2), kind=kOutput, calls=%fused_computation.13.clone.1 | convolution fusion | flops 118751232 | bytes 2146304 | tf_op jit(solution)/shard_map/while/body/eval_jaxpr/dot_general | solution.py:46
  94.2 3.3 %reshape.310 = bf16[64,256,32]{2,1,0:T(8,128)(2,1)} reshape(bf16[4096,128]{1,0:T(8,128)(2,1)S(1)} %fusion.126) | data formatting | bytes 2097152 | tf_op jit(solution)/shard_map/while/body/eval_jaxpr/reshape | solution.py:50
  98.2 3.5 %fusion.127 = f32[64,1,256]{2,1,0:T(1,128)S(1)} fusion(bf16[64,256,32]{2,1,0:T(8,128)(2,1)} %reshape.310, bf16[64,32,1]{1,0,2:T(8,128)(2,1)S(1)} %dynamic-slice_bitcast_fusion.2), kind=kOutput, calls=%fused_computation.48.clone.1 | convolution fusion | flops 1048576 | bytes 1118208 | tf_op jit(solution)/shard_map/while/body/eval_jaxpr/nqc,nc->nq/dot_general | solution.py:52
  105.2 1.3 multiply_reduce_fusion.3
  106.5 10.8 %fusion.126 = bf16[4096,128]{1,0:T(8,128)(2,1)S(1)} fusion(bf16[64,128]{1,0:T(8,128)(2,1)S(1)} %copy-done.9, f32[4096,64]{1,0:T(8,128)S(1)} %reshape.309, f32[4096]{0:T(1024)S(1)} %add_rsqrt_fusion.2, f32[4096]{0:T(1024)S(1)} %broadcast_multiply_fusion.2), kind=kOutput, calls=%fused_computation.13.clone.1 | convolution fusion | flops 118751232 | bytes 2146304 | tf_op jit(solution)/shard_map/while/body/eval_jaxpr/dot_general | solution.py:46
  117.3 3.3 %reshape.310 = bf16[64,256,32]{2,1,0:T(8,128)(2,1)} reshape(bf16[4096,128]{1,0:T(8,128)(2,1)S(1)} %fusion.126) | data formatting | bytes 2097152 | tf_op jit(solution)/shard_map/while/body/eval_jaxpr/reshape | solution.py:50
  121.3 3.5 %fusion.127 = f32[64,1,256]{2,1,0:T(1,128)S(1)} fusion(bf16[64,256,32]{2,1,0:T(8,128)(2,1)} %reshape.310, bf16[64,32,1]{1,0,2:T(8,128)(2,1)S(1)} %dynamic-slice_bitcast_fusion.2), kind=kOutput, calls=%fused_computation.48.clone.1 | convolution fusion | flops 1048576 | bytes 1118208 | tf_op jit(solution)/shard_map/while/body/eval_jaxpr/nqc,nc->nq/dot_general | solution.py:52
  128.3 1.3 multiply_reduce_fusion.3
  129.6 10.8 %fusion.126 = bf16[4096,128]{1,0:T(8,128)(2,1)S(1)} fusion(bf16[64,128]{1,0:T(8,128)(2,1)S(1)} %copy-done.9, f32[4096,64]{1,0:T(8,128)S(1)} %reshape.309, f32[4096]{0:T(1024)S(1)} %add_rsqrt_fusion.2, f32[4096]{0:T(1024)S(1)} %broadcast_multiply_fusion.2), kind=kOutput, calls=%fused_computation.13.clone.1 | convolution fusion | flops 118751232 | bytes 2146304 | tf_op jit(solution)/shard_map/while/body/eval_jaxpr/dot_general | solution.py:46
  140.5 3.3 %reshape.310 = bf16[64,256,32]{2,1,0:T(8,128)(2,1)} reshape(bf16[4096,128]{1,0:T(8,128)(2,1)S(1)} %fusion.126) | data formatting | bytes 2097152 | tf_op jit(solution)/shard_map/while/body/eval_jaxpr/reshape | solution.py:50
  144.5 3.5 %fusion.127 = f32[64,1,256]{2,1,0:T(1,128)S(1)} fusion(bf16[64,256,32]{2,1,0:T(8,128)(2,1)} %reshape.310, bf16[64,32,1]{1,0,2:T(8,128)(2,1)S(1)} %dynamic-slice_bitcast_fusion.2), kind=kOutput, calls=%fused_computation.48.clone.1 | convolution fusion | flops 1048576 | bytes 1118208 | tf_op jit(solution)/shard_map/while/body/eval_jaxpr/nqc,nc->nq/dot_general | solution.py:52
  151.4 1.3 multiply_reduce_fusion.3
  152.7 10.8 %fusion.126 = bf16[4096,128]{1,0:T(8,128)(2,1)S(1)} fusion(bf16[64,128]{1,0:T(8,128)(2,1)S(1)} %copy-done.9, f32[4096,64]{1,0:T(8,128)S(1)} %reshape.309, f32[4096]{0:T(1024)S(1)} %add_rsqrt_fusion.2, f32[4096]{0:T(1024)S(1)} %broadcast_multiply_fusion.2), kind=kOutput, calls=%fused_computation.13.clone.1 | convolution fusion | flops 118751232 | bytes 2146304 | tf_op jit(solution)/shard_map/while/body/eval_jaxpr/dot_general | solution.py:46
  163.6 3.3 %reshape.310 = bf16[64,256,32]{2,1,0:T(8,128)(2,1)} reshape(bf16[4096,128]{1,0:T(8,128)(2,1)S(1)} %fusion.126) | data formatting | bytes 2097152 | tf_op jit(solution)/shard_map/while/body/eval_jaxpr/reshape | solution.py:50
  167.6 3.5 %fusion.127 = f32[64,1,256]{2,1,0:T(1,128)S(1)} fusion(bf16[64,256,32]{2,1,0:T(8,128)(2,1)} %reshape.310, bf16[64,32,1]{1,0,2:T(8,128)(2,1)S(1)} %dynamic-slice_bitcast_fusion.2), kind=kOutput, calls=%fused_computation.48.clone.1 | convolution fusion | flops 1048576 | bytes 1118208 | tf_op jit(solution)/shard_map/while/body/eval_jaxpr/nqc,nc->nq/dot_general | solution.py:52
  172.0 11.3 %while.23 = (s32[]{:T(128)}, f32[76,256]{1,0:T(8,128)S(1)}, s32[4,64]{1,0:T(4,128)}, bf16[4,64,16,16]{1,3,2,0:T(8,128)(2,1)}, s32[4,64]{1,0:T(4,128)}, /*index=5*/s32[]{:T(128)}, s32[]{:T(128)}) while((s32[]{:T(128)}, f32[76,256]{1,0:T(8,128)S(1)}, s32[4,64]{1,0:T(4,128)}, bf16[4,64,16,16]{1,3,2,0:T(8,128)(2,1)}, ...), condition=%wide.region_9.10_spmd.clone.clone, body=%wide.region_8.9_spmd.clone.clone.sunk | while | flops 48877696 | bytes 1394271 | solution.py:114
  183.9 57.3 %all-reduce.3.cloned.1.call-done = f32[76,256]{1,0:T(8,128)} async-done(((f32[76,256]{1,0:T(8,128)}), f32[76,256]{1,0:T(8,128)}) %all-reduce.3.cloned.1.call-update) | async-done | bytes 77840 | tf_op jit(solution)/shard_map/psum | solution.py:187
  241.9 1.9 collective-permute-start.1
  243.8 5.2 %collective-permute-done.1 = f32[12,256]{1,0:T(8,128)S(1)} collective-permute-done((f32[12,256]{1,0:T(8,128)S(1)}, f32[12,256]{1,0:T(8,128)S(1)}, u32[]{:S(2)}, u32[]{:S(2)}) %collective-permute-start.1) | collective-permute-done | bytes 12320 | tf_op jit(solution)/shard_map/ppermute | solution.py:13
  249.0 1.5 slice_add_fusion
  (155 shorter events, 38.9 us)
Async XLA Ops:
  6.5 31.3 %copy-start = (bf16[256,256]{1,0:T(8,128)(2,1)S(1)}, bf16[256,256]{1,0:T(8,128)(2,1)}, u32[]{:S(2)}) copy-start(bf16[256,256]{1,0:T(8,128)(2,1)} %param.26) | copy-start | bytes 393220
  11.3 36.7 %all-to-all-start = ((s32[128,2,3]{2,1,0:T(2,128)}), s32[128,2,3]{2,1,0:T(2,128)S(1)}, u32[]{:S(2)}, u32[]{:S(2)}) async-start(s32[128,2,3]{2,1,0:T(2,128)} %bitcast.13), calls=%async_computation | async-start | bytes 262144 | tf_op jit(solution)/shard_map/all_to_all | solution.py:166
  30.8 28.4 %copy-start.4 = (bf16[16,64,256]{2,1,0:T(8,128)(2,1)S(1)}, bf16[16,64,256]{2,1,0:T(8,128)(2,1)}, u32[]{:S(2)}) copy-start(bf16[16,64,256]{2,1,0:T(8,128)(2,1)} %param.17) | copy-start | bytes 1572868
  31.8 27.4 %collective-permute-start = (bf16[3,64,256]{2,1,0:T(8,128)(2,1)S(1)}, bf16[3,64,256]{2,1,0:T(8,128)(2,1)S(1)}, u32[]{:S(2)}, u32[]{:S(2)}) collective-permute-start(bf16[3,64,256]{2,1,0:T(8,128)(2,1)S(1)} %slice.36), channel_id=1, source_target_pairs={{4,0},{8,4},{12,8},{16,12},{20,16},{24,20},{28,24},{32,28},{36,32}... | collective-permute-start | bytes 294920 | tf_op jit(solution)/shard_map/ppermute | solution.py:13
  48.0 31.4 %all-to-all-start.1 = ((bf16[128,2,32]{2,1,0:T(2,128)(2,1)}), bf16[128,2,32]{2,1,0:T(2,128)(2,1)}, u32[]{:S(2)}, u32[]{:S(2)}) async-start(bf16[128,2,32]{2,1,0:T(2,128)(2,1)} %bitcast.23), calls=%async_computation.1 | async-start | bytes 131072 | tf_op jit(solution)/shard_map/all_to_all | solution.py:165
  56.2 185.0 %all-reduce.3.cloned.1.call-start = ((), (), s32[]{:S(2)}) async-start(), calls=%async_computation.2 | async-start | bytes 163840 | tf_op jit(solution)/shard_map/psum | solution.py:187
  56.7 0.6 copy-start.7
  56.8 0.6 copy-start.8
  76.0 3.4 %copy-start.3 = (bf16[256,256]{1,0:T(8,128)(2,1)S(1)}, bf16[256,256]{1,0:T(8,128)(2,1)}, u32[]{:S(2)}) copy-start(bf16[256,256]{1,0:T(8,128)(2,1)} %param.28) | copy-start | bytes 393220
  79.4 92.5 %copy-start.5 = (f32[76,256]{1,0:T(8,128)S(1)}, f32[76,256]{1,0:T(8,128)}, u32[]{:S(2)}) copy-start(f32[76,256]{1,0:T(8,128)} %custom-call) | copy-start | bytes 233476
  79.4 1.3 copy-start.1
  81.4 1.9 copy-start.9
  98.2 4.3 %copy-start.2 = (bf16[4,64,4,4,256]{4,3,2,1,0:T(4,128)(2,1)S(1)}, bf16[4,64,4,4,256]{4,3,2,1,0:T(4,128)(2,1)}, u32[]{:S(2)}) copy-start(bf16[4,64,4,4,256]{4,3,2,1,0:T(4,128)(2,1)} %copy-done.1) | copy-start | bytes 6291460 | tf_op jit(solution)/shard_map/while
  102.6 1.3 copy-start.1
  104.5 1.9 copy-start.9
  121.3 4.4 %copy-start.2 = (bf16[4,64,4,4,256]{4,3,2,1,0:T(4,128)(2,1)S(1)}, bf16[4,64,4,4,256]{4,3,2,1,0:T(4,128)(2,1)}, u32[]{:S(2)}) copy-start(bf16[4,64,4,4,256]{4,3,2,1,0:T(4,128)(2,1)} %copy-done.1) | copy-start | bytes 6291460 | tf_op jit(solution)/shard_map/while
  125.7 1.3 copy-start.1
  127.7 1.9 copy-start.9
  144.5 4.4 %copy-start.2 = (bf16[4,64,4,4,256]{4,3,2,1,0:T(4,128)(2,1)S(1)}, bf16[4,64,4,4,256]{4,3,2,1,0:T(4,128)(2,1)}, u32[]{:S(2)}) copy-start(bf16[4,64,4,4,256]{4,3,2,1,0:T(4,128)(2,1)} %copy-done.1) | copy-start | bytes 6291460 | tf_op jit(solution)/shard_map/while
  148.8 1.3 copy-start.1
  150.8 1.9 copy-start.9
  167.6 4.4 %copy-start.2 = (bf16[4,64,4,4,256]{4,3,2,1,0:T(4,128)(2,1)S(1)}, bf16[4,64,4,4,256]{4,3,2,1,0:T(4,128)(2,1)}, u32[]{:S(2)}) copy-start(bf16[4,64,4,4,256]{4,3,2,1,0:T(4,128)(2,1)} %copy-done.1) | copy-start | bytes 6291460 | tf_op jit(solution)/shard_map/while
  183.2 0.6 copy-start.6
  241.9 7.2 %collective-permute-start.1 = (f32[12,256]{1,0:T(8,128)S(1)}, f32[12,256]{1,0:T(8,128)S(1)}, u32[]{:S(2)}, u32[]{:S(2)}) collective-permute-start(f32[12,256]{1,0:T(8,128)S(1)} %slice.51), channel_id=1, source_target_pairs={{0,4},{4,8},{8,12},{12,16},{16,20},{20,24},{24,28},{28,32},{32,36}... | collective-permute-start | bytes 36872 | tf_op jit(solution)/shard_map/ppermute | solution.py:13
Sparse Core Ops, SparseCore 0:
  184.0 57.0 all-reduce.2
where the time goes:
time: 258 us; the launch traced here: 257 us
  waiting for transfers between devices  69 us (27%)
  matrix products  64.2 us (25%)
  local copies, waits for them, and re-layouts  53.2 us (21%)
  starting transfers between devices  34.1 us (13%)
  other arithmetic  22.7 us (9%)
  between operations  13.6 us (5%)
    psum x1, waiting for transfers between devices, on_device(): summed = lax.psum(canvas, 'rep')  57.3 us
    dot_general x4, matrix products, mask_terms(): second = jnp.dot(active, conv_two, preferred_element_type=jnp.float32)  43.4 us
    all_to_all x1, starting transfers between devices, on_device(): lax.all_to_all(request_slots, 'tile', split_axis=0, concat_axis=0, tiled=...  19.5 us
    gather x2, local copies, waits for them, and re-layouts, cut_crops(): jnp.take(extended.reshape(height * width, channels), cell_index, axis=0)  16.7 us
    dot_general x4, matrix products, mask_terms(): jnp.einsum('nqc,nc->nq', upscaled, head_rows, preferred_element_type=jnp....  14 us
    reshape x4, local copies, waits for them, and re-layouts, mask_terms(): upscaled = jax.nn.gelu(second, approximate=False).astype(jnp.bfloat16).re...  13.1 us
    all_to_all x1, starting transfers between devices, on_device(): lax.all_to_all(head_slots, 'tile', split_axis=0, concat_axis=0, tiled=True)  8.16 us
    all_to_all x1, waiting for transfers between devices, on_device(): lax.all_to_all(request_slots, 'tile', split_axis=0, concat_axis=0, tiled=...  6.42 us
  transfers between devices with their start and end apart: 5, of which 3 were waited for; matrix products, arithmetic and copies ran while one was open for 11% of the time, Pallas kernels for 0%

commit v1 on v0

--- a/solution.py
+++ b/solution.py
@@ -184,7 +184,7 @@
         4 * strip_height + 4 * CK - 4,
         breadth,
     )
-    summed = lax.psum(canvas, "rep")
+    summed = jnp.sum(lax.all_gather(canvas, "rep"), axis=0)
     spilled = shifted(summed[4 * strip_height :], "tile", 1)
     return summed[: 4 * strip_height] + jnp.pad(
         spilled, ((0, 4 * strip_height - spilled.shape[0]), (0, 0))

time: 258 us -> 199 us (0.77)
  the two profiles are of different devices: /device:TPU:2 before, /device:TPU:6 now
where the time goes in v1:
time: 199 us; the launch traced here: 198 us
  matrix products  64.2 us (32%)
  local copies, waits for them, and re-layouts  51.9 us (26%)
  starting transfers between devices  35.8 us (18%)
  other arithmetic  21.8 us (11%)
  blocking collectives  12.9 us (6%)
  waiting for transfers between devices  10.2 us (5%)
    dot_general x4, matrix products, mask_terms(): second = jnp.dot(active, conv_two, preferred_element_type=jnp.float32)  43.4 us
    all_to_all x1, starting transfers between devices, on_device(): lax.all_to_all(request_slots, 'tile', split_axis=0, concat_axis=0, tiled=...  19.9 us
    gather x2, local copies, waits for them, and re-layouts, cut_crops(): jnp.take(extended.reshape(height * width, channels), cell_index, axis=0)  16.7 us
    dot_general x4, matrix products, mask_terms(): jnp.einsum('nqc,nc->nq', upscaled, head_rows, preferred_element_type=jnp....  14 us
    reshape x4, local copies, waits for them, and re-layouts, mask_terms(): upscaled = jax.nn.gelu(second, approximate=False).astype(jnp.bfloat16).re...  13.1 us
    all_gather x1, blocking collectives, on_device(): summed = jnp.sum(lax.all_gather(canvas, 'rep'), axis=0)  12.9 us
    all_to_all x1, starting transfers between devices, on_device(): lax.all_to_all(head_slots, 'tile', split_axis=0, concat_axis=0, tiled=True)  9.39 us
    ppermute x2, starting transfers between devices, shifted(): lax.ppermute(value, axis, [(source, source + steps) for source in range(l...  6.5 us
  transfers between devices with their start and end apart: 4, of which 2 were waited for; matrix products, arithmetic and copies ran while one was open for 15% of the time, Pallas kernels for 0%

profile of v1, /device:TPU:6, one launch (start us, length us, event | category | flops | bytes accessed | tf_op | source)
XLA Modules:
  0.0 197.6 jit_solution(7991645341286870856)
XLA Ops:
  3.3 1.5 scatter_custom_fusion
  4.7 19.9 %all-to-all-start = ((s32[128,2,3]{2,1,0:T(2,128)}), s32[128,2,3]{2,1,0:T(2,128)S(1)}, u32[]{:S(2)}, u32[]{:S(2)}) async-start(s32[128,2,3]{2,1,0:T(2,128)} %bitcast.13), calls=%async_computation | async-start | bytes 262144 | tf_op jit(solution)/shard_map/all_to_all | solution.py:166
  25.6 4.6 %collective-permute-start = (bf16[3,64,256]{2,1,0:T(8,128)(2,1)S(1)}, bf16[3,64,256]{2,1,0:T(8,128)(2,1)S(1)}, u32[]{:S(2)}, u32[]{:S(2)}) collective-permute-start(bf16[3,64,256]{2,1,0:T(8,128)(2,1)S(1)} %slice.36), channel_id=1, source_target_pairs={{4,0},{8,4},{12,8},{16,12},{20,16},{24,20},{28,24},{32,28},{36,32}... | collective-permute-start | bytes 294920 | tf_op jit(solution)/shard_map/ppermute | solution.py:13
  32.0 1.2 fusion.74
  34.2 1.5 scatter_custom_fusion.1
  35.7 5.0 %all-to-all-done = s32[128,2,3]{2,1,0:T(2,128)S(1)} async-done(((s32[128,2,3]{2,1,0:T(2,128)}), s32[128,2,3]{2,1,0:T(2,128)S(1)}, u32[]{:S(2)}, u32[]{:S(2)}) %all-to-all-start) | async-done | bytes 3104 | tf_op jit(solution)/shard_map/all_to_all | solution.py:166
  40.6 9.4 %all-to-all-start.1 = ((bf16[128,2,32]{2,1,0:T(2,128)(2,1)}), bf16[128,2,32]{2,1,0:T(2,128)(2,1)}, u32[]{:S(2)}, u32[]{:S(2)}) async-start(bf16[128,2,32]{2,1,0:T(2,128)(2,1)} %bitcast.23), calls=%async_computation.1 | async-start | bytes 131072 | tf_op jit(solution)/shard_map/all_to_all | solution.py:165
  52.9 14.6 %gather_fusion = bf16[4096,256]{1,0:T(8,128)(2,1)S(1)} fusion(bf16[1216,256]{1,0:T(8,128)(2,1)S(1)} %bitcast.79, s32[4096]{0:T(1024)S(1)} %broadcast_clamp_fusion), kind=kCustom, calls=%fused_computation | custom fusion | bytes 4210688 | tf_op jit(solution)/shard_map/jit(_take)/gather | solution.py:83
  67.5 2.1 %gather.7 = bf16[4,64,4,4,256]{4,3,2,1,0:T(4,128)(2,1)} reshape(bf16[4096,256]{1,0:T(8,128)(2,1)S(1)} %gather_fusion) | data formatting | bytes 4194304 | tf_op jit(solution)/shard_map/jit(_take)/gather | solution.py:83
  69.6 3.4 %broadcast_select_fusion = bf16[4,64,4,4,256]{4,3,2,1,0:T(4,128)(2,1)S(1)} fusion(bf16[4,64,4,4,256]{4,3,2,1,0:T(4,128)(2,1)} %gather.7, pred[4,64,4,4]{3,2,1,0:T(4,128)(4,1)S(1)} %copy.42), kind=kLoop, calls=%fused_computation.104 | loop fusion | flops 1048576 | bytes 4198400 | tf_op jit(solution)/shard_map/jit(_take)/select_n | solution.py:83
  73.1 92.5 %while.22 = (s32[]{:T(128)}, bf16[4,64,16,16]{1,3,2,0:T(8,128)(2,1)}, bf16[4,64,4,4,256]{4,3,2,1,0:T(4,128)(2,1)S(1)}, bf16[256,256]{1,0:T(8,128)(2,1)S(1)}, bf1...) while((s32[]{:T(128)}, ...), condition=%wide.region_7.8_spmd, body=%wide.region_4.7_spmd.sunk | while | flops 255102976 | bytes 30717376 | solution.py:66
  75.7 1.3 multiply_reduce_fusion.3
  77.0 10.8 %fusion.126 = bf16[4096,128]{1,0:T(8,128)(2,1)S(1)} fusion(bf16[64,128]{1,0:T(8,128)(2,1)S(1)} %copy-done.8, f32[4096,64]{1,0:T(8,128)S(1)} %reshape.313, f32[4096]{0:T(1024)S(1)} %add_rsqrt_fusion.2, f32[4096]{0:T(1024)S(1)} %broadcast_multiply_fusion.2), kind=kOutput, calls=%fused_computation.13.clone.1 | convolution fusion | flops 118751232 | bytes 2146304 | tf_op jit(solution)/shard_map/while/body/eval_jaxpr/dot_general | solution.py:46
  87.9 3.3 %reshape.314 = bf16[64,256,32]{2,1,0:T(8,128)(2,1)} reshape(bf16[4096,128]{1,0:T(8,128)(2,1)S(1)} %fusion.126) | data formatting | bytes 2097152 | tf_op jit(solution)/shard_map/while/body/eval_jaxpr/reshape | solution.py:50
  91.9 3.5 %fusion.127 = f32[64,1,256]{2,1,0:T(1,128)S(1)} fusion(bf16[64,256,32]{2,1,0:T(8,128)(2,1)} %reshape.314, bf16[64,32,1]{1,0,2:T(8,128)(2,1)S(1)} %dynamic-slice_bitcast_fusion.2), kind=kOutput, calls=%fused_computation.48.clone.1 | convolution fusion | flops 1048576 | bytes 1118208 | tf_op jit(solution)/shard_map/while/body/eval_jaxpr/nqc,nc->nq/dot_general | solution.py:52
  96.5 1.0 copy-done.1
  98.8 1.3 multiply_reduce_fusion.3
  100.1 10.8 %fusion.126 = bf16[4096,128]{1,0:T(8,128)(2,1)S(1)} fusion(bf16[64,128]{1,0:T(8,128)(2,1)S(1)} %copy-done.8, f32[4096,64]{1,0:T(8,128)S(1)} %reshape.313, f32[4096]{0:T(1024)S(1)} %add_rsqrt_fusion.2, f32[4096]{0:T(1024)S(1)} %broadcast_multiply_fusion.2), kind=kOutput, calls=%fused_computation.13.clone.1 | convolution fusion | flops 118751232 | bytes 2146304 | tf_op jit(solution)/shard_map/while/body/eval_jaxpr/dot_general | solution.py:46
  111.0 3.3 %reshape.314 = bf16[64,256,32]{2,1,0:T(8,128)(2,1)} reshape(bf16[4096,128]{1,0:T(8,128)(2,1)S(1)} %fusion.126) | data formatting | bytes 2097152 | tf_op jit(solution)/shard_map/while/body/eval_jaxpr/reshape | solution.py:50
  115.0 3.5 %fusion.127 = f32[64,1,256]{2,1,0:T(1,128)S(1)} fusion(bf16[64,256,32]{2,1,0:T(8,128)(2,1)} %reshape.314, bf16[64,32,1]{1,0,2:T(8,128)(2,1)S(1)} %dynamic-slice_bitcast_fusion.2), kind=kOutput, calls=%fused_computation.48.clone.1 | convolution fusion | flops 1048576 | bytes 1118208 | tf_op jit(solution)/shard_map/while/body/eval_jaxpr/nqc,nc->nq/dot_general | solution.py:52
  121.9 1.3 multiply_reduce_fusion.3
  123.3 10.8 %fusion.126 = bf16[4096,128]{1,0:T(8,128)(2,1)S(1)} fusion(bf16[64,128]{1,0:T(8,128)(2,1)S(1)} %copy-done.8, f32[4096,64]{1,0:T(8,128)S(1)} %reshape.313, f32[4096]{0:T(1024)S(1)} %add_rsqrt_fusion.2, f32[4096]{0:T(1024)S(1)} %broadcast_multiply_fusion.2), kind=kOutput, calls=%fused_computation.13.clone.1 | convolution fusion | flops 118751232 | bytes 2146304 | tf_op jit(solution)/shard_map/while/body/eval_jaxpr/dot_general | solution.py:46
  134.1 3.3 %reshape.314 = bf16[64,256,32]{2,1,0:T(8,128)(2,1)} reshape(bf16[4096,128]{1,0:T(8,128)(2,1)S(1)} %fusion.126) | data formatting | bytes 2097152 | tf_op jit(solution)/shard_map/while/body/eval_jaxpr/reshape | solution.py:50
  138.1 3.5 %fusion.127 = f32[64,1,256]{2,1,0:T(1,128)S(1)} fusion(bf16[64,256,32]{2,1,0:T(8,128)(2,1)} %reshape.314, bf16[64,32,1]{1,0,2:T(8,128)(2,1)S(1)} %dynamic-slice_bitcast_fusion.2), kind=kOutput, calls=%fused_computation.48.clone.1 | convolution fusion | flops 1048576 | bytes 1118208 | tf_op jit(solution)/shard_map/while/body/eval_jaxpr/nqc,nc->nq/dot_general | solution.py:52
  145.1 1.3 multiply_reduce_fusion.3
  146.4 10.8 %fusion.126 = bf16[4096,128]{1,0:T(8,128)(2,1)S(1)} fusion(bf16[64,128]{1,0:T(8,128)(2,1)S(1)} %copy-done.8, f32[4096,64]{1,0:T(8,128)S(1)} %reshape.313, f32[4096]{0:T(1024)S(1)} %add_rsqrt_fusion.2, f32[4096]{0:T(1024)S(1)} %broadcast_multiply_fusion.2), kind=kOutput, calls=%fused_computation.13.clone.1 | convolution fusion | flops 118751232 | bytes 2146304 | tf_op jit(solution)/shard_map/while/body/eval_jaxpr/dot_general | solution.py:46
  157.2 3.3 %reshape.314 = bf16[64,256,32]{2,1,0:T(8,128)(2,1)} reshape(bf16[4096,128]{1,0:T(8,128)(2,1)S(1)} %fusion.126) | data formatting | bytes 2097152 | tf_op jit(solution)/shard_map/while/body/eval_jaxpr/reshape | solution.py:50
  161.2 3.5 %fusion.127 = f32[64,1,256]{2,1,0:T(1,128)S(1)} fusion(bf16[64,256,32]{2,1,0:T(8,128)(2,1)} %reshape.314, bf16[64,32,1]{1,0,2:T(8,128)(2,1)S(1)} %dynamic-slice_bitcast_fusion.2), kind=kOutput, calls=%fused_computation.48.clone.1 | convolution fusion | flops 1048576 | bytes 1118208 | tf_op jit(solution)/shard_map/while/body/eval_jaxpr/nqc,nc->nq/dot_general | solution.py:52
  165.6 11.3 %while.23 = (s32[]{:T(128)}, f32[76,256]{1,0:T(8,128)S(1)}, s32[4,64]{1,0:T(4,128)}, bf16[4,64,16,16]{1,3,2,0:T(8,128)(2,1)}, s32[4,64]{1,0:T(4,128)}, /*index=5*/s32[]{:T(128)}, s32[]{:T(128)}) while((s32[]{:T(128)}, f32[76,256]{1,0:T(8,128)S(1)}, s32[4,64]{1,0:T(4,128)}, bf16[4,64,16,16]{1,3,2,0:T(8,128)(2,1)}, ...), condition=%wide.region_9.10_spmd.clone.clone, body=%wide.region_8.9_spmd.clone.clone.sunk | while | flops 48877696 | bytes 1394271 | solution.py:114
  176.9 12.9 %all-gather.1 = f32[4,76,256]{2,1,0:T(8,128)S(1)} all-gather(f32[1,76,256]{2,1,0:T(8,128)S(1)} %bitcast.83), channel_id=2, replica_groups=mesh['tile'=128,'rep'=4] {'rep'}, dimensions={0}, use_global_device_ids=true | all-gather | bytes 389120 | tf_op jit(solution)/shard_map/all_gather | solution.py:187
  189.8 1.9 collective-permute-start.1
  191.7 5.2 %collective-permute-done.1 = f32[12,256]{1,0:T(8,128)S(1)} collective-permute-done((f32[12,256]{1,0:T(8,128)S(1)}, f32[12,256]{1,0:T(8,128)S(1)}, u32[]{:S(2)}, u32[]{:S(2)}) %collective-permute-start.1) | collective-permute-done | bytes 12320 | tf_op jit(solution)/shard_map/ppermute | solution.py:13
  (152 shorter events, 37.0 us)
Async XLA Ops:
  0.0 32.0 %copy-start = (bf16[256,256]{1,0:T(8,128)(2,1)S(1)}, bf16[256,256]{1,0:T(8,128)(2,1)}, u32[]{:S(2)}) copy-start(bf16[256,256]{1,0:T(8,128)(2,1)} %param.26) | copy-start | bytes 393220
  4.7 35.9 %all-to-all-start = ((s32[128,2,3]{2,1,0:T(2,128)}), s32[128,2,3]{2,1,0:T(2,128)S(1)}, u32[]{:S(2)}, u32[]{:S(2)}) async-start(s32[128,2,3]{2,1,0:T(2,128)} %bitcast.13), calls=%async_computation | async-start | bytes 262144 | tf_op jit(solution)/shard_map/all_to_all | solution.py:166
  24.6 28.2 %copy-start.4 = (bf16[16,64,256]{2,1,0:T(8,128)(2,1)S(1)}, bf16[16,64,256]{2,1,0:T(8,128)(2,1)}, u32[]{:S(2)}) copy-start(bf16[16,64,256]{2,1,0:T(8,128)(2,1)} %param.17) | copy-start | bytes 1572868
  25.6 27.2 %collective-permute-start = (bf16[3,64,256]{2,1,0:T(8,128)(2,1)S(1)}, bf16[3,64,256]{2,1,0:T(8,128)(2,1)S(1)}, u32[]{:S(2)}, u32[]{:S(2)}) collective-permute-start(bf16[3,64,256]{2,1,0:T(8,128)(2,1)S(1)} %slice.36), channel_id=1, source_target_pairs={{4,0},{8,4},{12,8},{16,12},{20,16},{24,20},{28,24},{32,28},{36,32}... | collective-permute-start | bytes 294920 | tf_op jit(solution)/shard_map/ppermute | solution.py:13
  40.6 32.4 %all-to-all-start.1 = ((bf16[128,2,32]{2,1,0:T(2,128)(2,1)}), bf16[128,2,32]{2,1,0:T(2,128)(2,1)}, u32[]{:S(2)}, u32[]{:S(2)}) async-start(bf16[128,2,32]{2,1,0:T(2,128)(2,1)} %bitcast.23), calls=%async_computation.1 | async-start | bytes 131072 | tf_op jit(solution)/shard_map/all_to_all | solution.py:165
  50.4 0.6 copy-start.6
  50.5 0.6 copy-start.7
  69.6 3.4 %copy-start.3 = (bf16[256,256]{1,0:T(8,128)(2,1)S(1)}, bf16[256,256]{1,0:T(8,128)(2,1)}, u32[]{:S(2)}) copy-start(bf16[256,256]{1,0:T(8,128)(2,1)} %param.28) | copy-start | bytes 393220
  73.1 92.5 %copy-start.5 = (f32[76,256]{1,0:T(8,128)S(1)}, f32[76,256]{1,0:T(8,128)}, u32[]{:S(2)}) copy-start(f32[76,256]{1,0:T(8,128)} %custom-call) | copy-start | bytes 233476
  73.1 1.3 copy-start.1
  75.1 1.9 copy-start.8
  91.9 4.3 %copy-start.2 = (bf16[4,64,4,4,256]{4,3,2,1,0:T(4,128)(2,1)S(1)}, bf16[4,64,4,4,256]{4,3,2,1,0:T(4,128)(2,1)}, u32[]{:S(2)}) copy-start(bf16[4,64,4,4,256]{4,3,2,1,0:T(4,128)(2,1)} %copy-done.1) | copy-start | bytes 6291460 | tf_op jit(solution)/shard_map/while
  96.2 1.3 copy-start.1
  98.2 1.9 copy-start.8
  115.0 4.3 %copy-start.2 = (bf16[4,64,4,4,256]{4,3,2,1,0:T(4,128)(2,1)S(1)}, bf16[4,64,4,4,256]{4,3,2,1,0:T(4,128)(2,1)}, u32[]{:S(2)}) copy-start(bf16[4,64,4,4,256]{4,3,2,1,0:T(4,128)(2,1)} %copy-done.1) | copy-start | bytes 6291460 | tf_op jit(solution)/shard_map/while
  119.3 1.3 copy-start.1
  121.3 1.9 copy-start.8
  138.1 4.3 %copy-start.2 = (bf16[4,64,4,4,256]{4,3,2,1,0:T(4,128)(2,1)S(1)}, bf16[4,64,4,4,256]{4,3,2,1,0:T(4,128)(2,1)}, u32[]{:S(2)}) copy-start(bf16[4,64,4,4,256]{4,3,2,1,0:T(4,128)(2,1)} %copy-done.1) | copy-start | bytes 6291460 | tf_op jit(solution)/shard_map/while
  142.5 1.3 copy-start.1
  144.4 1.9 copy-start.8
  161.2 4.3 %copy-start.2 = (bf16[4,64,4,4,256]{4,3,2,1,0:T(4,128)(2,1)S(1)}, bf16[4,64,4,4,256]{4,3,2,1,0:T(4,128)(2,1)}, u32[]{:S(2)}) copy-start(bf16[4,64,4,4,256]{4,3,2,1,0:T(4,128)(2,1)} %copy-done.1) | copy-start | bytes 6291460 | tf_op jit(solution)/shard_map/while
  189.8 7.2 %collective-permute-start.1 = (f32[12,256]{1,0:T(8,128)S(1)}, f32[12,256]{1,0:T(8,128)S(1)}, u32[]{:S(2)}, u32[]{:S(2)}) collective-permute-start(f32[12,256]{1,0:T(8,128)S(1)} %slice.51), channel_id=1, source_target_pairs={{0,4},{4,8},{8,12},{12,16},{16,20},{20,24},{24,28},{28,32},{32,36}... | collective-permute-start | bytes 36872 | tf_op jit(solution)/shard_map/ppermute | solution.py:13
